TPU v7x, 32 devices: a whole 2x2x4 slice. The times are simulated.
32 devices in a mesh: dp: 16 (over z, y, core), tensor: 2 (over x).
Axes of the slice: x: 2, y: 2, z: 4, core: 2. Of those that a mesh axis runs over, the one named last changes fastest.
Arguments:
- block_input: bfloat16 [160, 197, 768], P('dp'), may hold values from -6 to 6
- image_counts: int32 [16], P('dp'), may hold values from 1 to 10, 88 in all
- first_norm_gain: float32 [768], replicated, may hold values from 0.1 to 1.9
- first_norm_bias: float32 [768], replicated, may hold values from -3 to 3
- w_qkv: bfloat16 [3, 768, 768], P(None, None, 'tensor'), may hold values from -8 to 8
- qv_bias: float32 [2, 768], P(None, 'tensor'), may hold values from -3 to 3
- w_out: bfloat16 [768, 768], P('tensor'), may hold values from -0.75 to 0.75
- b_out: float32 [768], replicated, may hold values from -3 to 3
- second_norm_gain: float32 [768], replicated, may hold values from 0.1 to 1.9
- second_norm_bias: float32 [768], replicated, may hold values from -3 to 3
- w_fc1: bfloat16 [768, 3072], P(None, 'tensor'), may hold values from -0.21875 to 0.21875
- b_fc1: float32 [3072], P('tensor'), may hold values from -3 to 3
- w_fc2: bfloat16 [3072, 768], P('tensor'), may hold values from -0.109375 to 0.109375
- b_fc2: float32 [768], replicated, may hold values from -3 to 3
- cotangent: bfloat16 [160, 197, 768], P('dp'), may hold values from -6 to 6
Outputs:
- block_out: bfloat16 [160, 197, 768], P('dp')
- gradient_of_input: bfloat16 [160, 197, 768], P('dp')
- first_norm_gain_gradient: float32 [768], replicated
- grad_ln1_bias: float32 [768], replicated
- grad_w_qkv: float32 [3, 768, 768], P(None, None, 'tensor')
- grad_qv_bias: float32 [2, 768], P(None, 'tensor')
- grad_w_out: float32 [768, 768], P('tensor')
- grad_b_out: float32 [768], replicated
- second_norm_gain_gradient: float32 [768], replicated
- grad_ln2_bias: float32 [768], replicated
- grad_w_fc1: float32 [768, 3072], P(None, 'tensor')
- grad_b_fc1: float32 [3072], P('tensor')
- grad_w_fc2: float32 [3072, 768], P('tensor')
- grad_b_fc2: float32 [768], replicated
All inputs are finite; a program needn't handle non-finite values. No bound on the sum of `image_counts` on one device may be relied on, other than what follows from the above.
Results may differ from a plain program's by a relative error of at most 0.012.
The roundings to bfloat16 on the way count: a program that leaves them out, or rounds other values in their place, can miss the bound.
Values sent between devices are 32-bit elements; how exact they have to be, the bound alone decides.
No kernel may reach another device: no remote copies, remote signals or barrier semaphores. Data moves between devices by JAX's collectives and lax.ppermute only.
A program may use at most 256 MiB of HBM per device.

v0:
```python
import jax
import jax.numpy as jnp
from jax import lax
from jax.sharding import PartitionSpec as P

HD = 64
EPSILON = 1e-06
INV_ROOT2 = 0.7071067811865476
INV_ROOT2PI = 0.3989422804014327


def apply_layer_norm(values, norm_gain, norm_bias):
    center = jnp.mean(values, -1, keepdims=True)
    shifted = values - center
    spread = jnp.mean(shifted * shifted, -1, keepdims=True)
    inv_std = lax.rsqrt(spread + EPSILON)
    normed = shifted * inv_std
    return (normed * norm_gain + norm_bias, normed, inv_std)


def norm_backward_pass(grad_normed, normed, inv_std, norm_gain):
    scaled = grad_normed * norm_gain
    first = jnp.mean(scaled, -1, keepdims=True)
    second = jnp.mean(scaled * normed, -1, keepdims=True)
    return inv_std * (scaled - first - normed * second)


def gelu_value(pre_act):
    return 0.5 * pre_act * (1.0 + lax.erf(pre_act * INV_ROOT2))


def gelu_slope(pre_act):
    return (
        0.5 * (1.0 + lax.erf(pre_act * INV_ROOT2))
        + pre_act * jnp.exp(-0.5 * pre_act * pre_act) * INV_ROOT2PI
    )


def head_scores(queries, keys_all, scale):
    return (
        jnp.einsum("ishd,ithd->ihst", queries, keys_all, preferred_element_type=jnp.float32) * scale
    )


def shards(
    block_input,
    image_counts,
    first_norm_gain,
    first_norm_bias,
    w_qkv,
    qv_bias,
    w_out,
    b_out,
    second_norm_gain,
    second_norm_bias,
    w_fc1,
    b_fc1,
    w_fc2,
    b_fc2,
    cotangent,
):
    float_thirtytwo = jnp.float32
    bfloat_sixteen = jnp.bfloat16
    image_batch, sequence_length, model_width = block_input.shape
    total_rows = image_batch * sequence_length
    local_heads = w_qkv.shape[2] // HD
    local_width = local_heads * HD
    scale = HD ** (-0.5)
    shape4 = (image_batch, sequence_length, local_heads, HD)
    live_rows = (jnp.arange(total_rows, dtype=jnp.int32) // sequence_length < image_counts[0])[
        :, None
    ]
    input_tokens = block_input.reshape(total_rows, model_width).astype(float_thirtytwo)
    first_normed_tokens, first_centered_scaled, first_inverse_deviation = apply_layer_norm(
        input_tokens, first_norm_gain, first_norm_bias
    )
    normed_one_b = first_normed_tokens.astype(bfloat_sixteen)
    projected = jnp.einsum(
        "nd,cde->cne", normed_one_b, w_qkv, preferred_element_type=float_thirtytwo
    )
    queries = (projected[0] + qv_bias[0]).astype(bfloat_sixteen).reshape(shape4)
    keys_all = projected[1].astype(bfloat_sixteen).reshape(shape4)
    values_all = (projected[2] + qv_bias[1]).astype(bfloat_sixteen).reshape(shape4)
    scores = head_scores(queries, keys_all, scale)
    log_total = jax.nn.logsumexp(scores, axis=-1)
    probs = jnp.exp(scores - log_total[..., None]).astype(bfloat_sixteen)
    context = (
        jnp.einsum("ihst,ithd->ishd", probs, values_all, preferred_element_type=float_thirtytwo)
        .astype(bfloat_sixteen)
        .reshape(total_rows, local_width)
    )
    attn_part = jnp.dot(context, w_out, preferred_element_type=float_thirtytwo)
    attn_full = lax.psum(attn_part, "tensor")
    residual_stream = input_tokens + (attn_full + b_out)
    second_normed_tokens, second_centered_scaled, second_inverse_deviation = apply_layer_norm(
        residual_stream, second_norm_gain, second_norm_bias
    )
    normed_two_b = second_normed_tokens.astype(bfloat_sixteen)
    pre_act = jnp.dot(normed_two_b, w_fc1, preferred_element_type=float_thirtytwo) + b_fc1
    activated = gelu_value(pre_act).astype(bfloat_sixteen)
    mlp_part = jnp.dot(activated, w_fc2, preferred_element_type=float_thirtytwo)
    mlp_full = lax.psum(mlp_part, "tensor")
    outputs = residual_stream + (mlp_full + b_fc2)
    block_out = (
        jnp.where(live_rows, outputs, 0.0)
        .astype(bfloat_sixteen)
        .reshape(image_batch, sequence_length, model_width)
    )
    output_gradient = jnp.where(
        live_rows, cotangent.reshape(total_rows, model_width), jnp.zeros((), bfloat_sixteen)
    )
    grad_w_fc2 = jnp.einsum(
        "nf,nd->fd", activated, output_gradient, preferred_element_type=float_thirtytwo
    )
    grad_b_fc2 = jnp.sum(output_gradient.astype(float_thirtytwo), axis=0)
    grad_act = jnp.einsum(
        "nd,fd->nf", output_gradient, w_fc2, preferred_element_type=float_thirtytwo
    )
    grad_pre = (grad_act * gelu_slope(pre_act)).astype(bfloat_sixteen)
    grad_w_fc1 = jnp.einsum(
        "nd,nf->df", normed_two_b, grad_pre, preferred_element_type=float_thirtytwo
    )
    grad_b_fc1 = jnp.sum(grad_pre.astype(float_thirtytwo), axis=0)
    norm_two_part = jnp.einsum("nf,df->nd", grad_pre, w_fc1, preferred_element_type=float_thirtytwo)
    second_normed_gradient = lax.psum(norm_two_part, "tensor")
    second_norm_gain_gradient = jnp.sum(second_normed_gradient * second_centered_scaled, axis=0)
    grad_ln2_bias = jnp.sum(second_normed_gradient, axis=0)
    residual_gradient = output_gradient.astype(float_thirtytwo) + norm_backward_pass(
        second_normed_gradient, second_centered_scaled, second_inverse_deviation, second_norm_gain
    )
    grad_resid_b = residual_gradient.astype(bfloat_sixteen)
    grad_w_out = jnp.einsum(
        "ne,nd->ed", context, grad_resid_b, preferred_element_type=float_thirtytwo
    )
    grad_b_out = jnp.sum(residual_gradient, axis=0)
    grad_context = (
        jnp.einsum("nd,ed->ne", grad_resid_b, w_out, preferred_element_type=float_thirtytwo)
        .astype(bfloat_sixteen)
        .reshape(shape4)
    )
    probs_full = jnp.exp(head_scores(queries, keys_all, scale) - log_total[..., None])
    probs_again = probs_full.astype(bfloat_sixteen)
    grad_values = jnp.einsum(
        "ihst,ishd->ithd", probs_again, grad_context, preferred_element_type=float_thirtytwo
    ).astype(bfloat_sixteen)
    grad_probs = jnp.einsum(
        "ishd,ithd->ihst", grad_context, values_all, preferred_element_type=float_thirtytwo
    )
    row_dot = jnp.sum(probs_full * grad_probs, axis=-1, keepdims=True)
    grad_scores = (probs_full * (grad_probs - row_dot)).astype(bfloat_sixteen)
    grad_queries = (
        jnp.einsum("ihst,ithd->ishd", grad_scores, keys_all, preferred_element_type=float_thirtytwo)
        * scale
    ).astype(bfloat_sixteen)
    grad_keys = (
        jnp.einsum("ihst,ishd->ithd", grad_scores, queries, preferred_element_type=float_thirtytwo)
        * scale
    ).astype(bfloat_sixteen)
    grad_proj = jnp.stack([grad_queries, grad_keys, grad_values]).reshape(
        3, total_rows, local_width
    )
    grad_w_qkv = jnp.einsum(
        "nd,cne->cde", normed_one_b, grad_proj, preferred_element_type=float_thirtytwo
    )
    grad_qv_bias = jnp.stack(
        [
            jnp.sum(grad_proj[0].astype(float_thirtytwo), axis=0),
            jnp.sum(grad_proj[2].astype(float_thirtytwo), axis=0),
        ]
    )
    norm_one_part = jnp.einsum(
        "cne,cde->nd", grad_proj, w_qkv, preferred_element_type=float_thirtytwo
    )
    first_normed_gradient = lax.psum(norm_one_part, "tensor")
    first_norm_gain_gradient = jnp.sum(first_normed_gradient * first_centered_scaled, axis=0)
    grad_ln1_bias = jnp.sum(first_normed_gradient, axis=0)
    gradient_of_input = (
        (
            residual_gradient
            + norm_backward_pass(
                first_normed_gradient,
                first_centered_scaled,
                first_inverse_deviation,
                first_norm_gain,
            )
        )
        .astype(bfloat_sixteen)
        .reshape(image_batch, sequence_length, model_width)
    )
    summed = lax.psum(
        (
            first_norm_gain_gradient,
            grad_ln1_bias,
            grad_w_qkv,
            grad_qv_bias,
            grad_w_out,
            grad_b_out,
            second_norm_gain_gradient,
            grad_ln2_bias,
            grad_w_fc1,
            grad_b_fc1,
            grad_w_fc2,
            grad_b_fc2,
        ),
        "dp",
    )
    first_norm_gain_gradient, grad_ln1_bias, grad_w_qkv, grad_qv_bias, grad_w_out, grad_b_out = (
        summed[0],
        summed[1],
        summed[2],
        summed[3],
        summed[4],
        summed[5],
    )
    second_norm_gain_gradient, grad_ln2_bias, grad_w_fc1, grad_b_fc1, grad_w_fc2, grad_b_fc2 = (
        summed[6],
        summed[7],
        summed[8],
        summed[9],
        summed[10],
        summed[11],
    )
    return (
        block_out,
        gradient_of_input,
        first_norm_gain_gradient,
        grad_ln1_bias,
        grad_w_qkv,
        grad_qv_bias,
        grad_w_out,
        grad_b_out,
        second_norm_gain_gradient,
        grad_ln2_bias,
        grad_w_fc1,
        grad_b_fc1,
        grad_w_fc2,
        grad_b_fc2,
    )


def solution(mesh):
    in_specs = (
        P("dp", None, None),
        P("dp"),
        P(),
        P(),
        P(None, None, "tensor"),
        P(None, "tensor"),
        P("tensor", None),
        P(),
        P(),
        P(),
        P(None, "tensor"),
        P("tensor"),
        P("tensor", None),
        P(),
        P("dp", None, None),
    )
    out_specs = (
        P("dp", None, None),
        P("dp", None, None),
        P(),
        P(),
        P(None, None, "tensor"),
        P(None, "tensor"),
        P("tensor", None),
        P(),
        P(),
        P(),
        P(None, "tensor"),
        P("tensor"),
        P("tensor", None),
        P(),
    )
    return jax.shard_map(shards, mesh=mesh, in_specs=in_specs, out_specs=out_specs, check_vma=False)
```

profile of v0, /device:TPU:0, one launch (start us, length us, event | category | flops | bytes accessed | tf_op | source)
XLA Modules:
  0.0 1190.0 jit_solution(15098997224716500326)
XLA Ops:
  7.3 6.9 reshape.188
  19.7 7.4 convolution_bitcast_fusion
  35.0 8.1 squeeze.14
  68.9 8.1 squeeze.13
  80.2 8.9 convert_bitcast_fusion.1
  92.1 5.9 reshape.183
  108.5 146.6 %all-reduce.8.cloned.1.call-done = f32[1970,768]{1,0:T(8,128)} async-done(((f32[1970,768]{1,0:T(8,128)}), f32[1970,768]{1,0:T(8,128)}) %all-reduce.8.cloned.1.call-update) | async-done | bytes 6051856 | tf_op jit(solution)/shard_map/psum | solution.py:93
  261.3 8.0 multiply_convert_fusion.1
  269.4 9.3 convert_reduce_fusion
  281.2 6.8 fusion.39
  288.1 10.1 fusion.29
  298.2 8.9 fusion.32
  307.1 130.0 %all-reduce.10.cloned.1.call-done = f32[1970,768]{1,0:T(8,128)} async-done(((f32[1970,768]{1,0:T(8,128)}), f32[1970,768]{1,0:T(8,128)}) %all-reduce.10.cloned.1.call-update) | async-done | bytes 6051856 | tf_op jit(solution)/shard_map/psum | solution.py:125
  437.2 6.0 multiply_reduce_fusion.3
  444.3 5.8 fusion.34
  464.0 8.5 convert_reduce_fusion.2
  472.5 12.1 %multiply_reduce_fusion = (f32[10,6,197]{2,1,0:T(8,128)S(1)}, f32[10,6,197,197]{2,3,1,0:T(8,128)}) fusion(f32[10,6,197,197]{2,3,1,0:T(8,128)} %copy-done.2, f32[10,6,197]{2,1,0:T(8,128)S(1)} %log_add_fusion, bf16[10,197,6,64]{1,3,2,0:T(8,128)(2,1)S(1)} %copy.49, bf16[10,197,6,64]{1,0,3,2:T(8,128)(2,1)} %copy-done.11), kind=kOutput, calls=%fused_computation.2 | convolution fusion | flops 307355456 | bytes 21748800 | tf_op jit(solution)/shard_map/ishd,ithd->ihst/dot_general | solution.py:146
  484.6 6.5 multiply_convert_fusion
  498.9 5.8 copy.70
  504.6 6.0 reshape.193
  510.6 5.9 copy.69
  516.5 6.0 reshape.192
  526.9 6.1 reshape.191
  538.6 9.1 convolution_bitcast_fusion.2
  547.8 11.2 fusion.38
  559.0 6.2 convolution_bitcast_fusion.1
  567.7 236.9 %all-reduce.12.cloned.1.call-done = (f32[3,768,384]{1,2,0:T(8,128)}, f32[384,768]{1,0:T(8,128)}, f32[768,1536]{1,0:T(8,128)}, f32[1536,768]{1,0:T(8,128)}) async-done(((f32[3,768,384]{1,2,0:T(8,128)}, f32[384,768]{1,0:T(8,128)}, f32[768,1536]{1,0:T(8,128)}, f32[1536,768]{1,0:T(8,128)}), (f32[3,768,384]{1,2,0:T(8,128)}, f32[384,768]{1,0:T(8,128)}, f32[768,1536]{1,0:T(8,128)}, ...) | async-done | bytes 14155792 | tf_op jit(solution)/shard_map/psum | solution.py:190
  809.7 275.8 %all-reduce.14.cloned.1.call-done = (f32[1970,768]{1,0:T(8,128)}, f32[1970,768]{1,0:T(8,128)}) async-done(((f32[1970,768]{1,0:T(8,128)}, f32[1970,768]{1,0:T(8,128)}), (f32[1970,768]{1,0:T(8,128)}, f32[1970,768]{1,0:T(8,128)})) %all-reduce.14.cloned.1.call-update) | async-done | bytes 12103696 | tf_op jit(solution)/shard_map/psum | solution.py:102
  1085.6 5.9 multiply_reduce_fusion.4
  1091.8 6.7 add_convert_fusion.2
  1102.6 6.6 select_convert_fusion
  1113.3 61.7 %all-reduce = (f32[768]{0:T(1024)}, f32[768]{0:T(1024)}, f32[2,384]{1,0:T(2,128)}, f32[768]{0:T(1024)}, f32[768]{0:T(1024)}, /*index=5*/f32[768]{0:T(1024)}, f32[1536]{0:T(1024)}, f32[768]{0:T(1024)}) all-reduce(f32[768]{0:T(1024)S(1)} %get-tuple-element.44, ...), channel_id=1, replica_groups=mesh['dp'=16,'tensor'=2] {'dp'}, use_global_device_ids=true, to_apply=%region_16.17 | all-reduce | flops 6912 | bytes 55296 | tf_op jit(solution)/shard_map/psum | solution.py:190
  (149 shorter events, 121.0 us)
Async XLA Ops:
  7.2 254.1 %copy-start = (bf16[768,1536]{1,0:T(8,128)(2,1)S(1)}, bf16[768,1536]{1,0:T(8,128)(2,1)}, u32[]{:S(2)}) copy-start(bf16[768,1536]{1,0:T(8,128)(2,1)} %param.25) | copy-start | bytes 7077892
  7.2 12.5 %copy-start.24 = (f32[768]{0:T(1024)S(1)}, f32[768]{0:T(1024)}, u32[]{:S(2)}) copy-start(f32[768]{0:T(1024)} %param.17) | copy-start | bytes 9220
  7.2 12.5 %copy-start.34 = (f32[768]{0:T(1024)S(1)}, f32[768]{0:T(1024)}, u32[]{:S(2)}) copy-start(f32[768]{0:T(1024)} %param.18) | copy-start | bytes 9220
  7.2 247.9 %all-reduce.8.cloned.1.call-start = ((), (), s32[]{:S(2)}) async-start(), calls=%async_computation | async-start | bytes 12140544 | tf_op jit(solution)/shard_map/psum | solution.py:93
  19.5 7.6 copy-start.20
  19.7 7.5 copy-start.22
  35.0 8.1 copy-start.29
  80.1 8.9 copy-start.11
  89.0 9.0 copy-start.16
  103.7 151.4 %copy-start.27 = (f32[768]{0:T(1024)S(1)}, f32[768]{0:T(1024)}, u32[]{:S(2)}) copy-start(f32[768]{0:T(1024)} %param.22) | copy-start | bytes 9220
  103.8 333.4 %all-reduce.10.cloned.1.call-start = ((), (), s32[]{:S(2)}) async-start(), calls=%async_computation.1 | async-start | bytes 12140544 | tf_op jit(solution)/shard_map/psum | solution.py:125
  260.4 9.0 copy-start.3
  261.3 8.1 copy-start.13
  261.3 8.1 copy-start.30
  288.0 516.6 %all-reduce.12.cloned.1.call-start = ((), (), s32[]{:S(2)}) async-start(), calls=%async_computation.2 | async-start | bytes 28311552 | tf_op jit(solution)/shard_map/psum | solution.py:190
  288.1 10.2 copy-start.37
  437.2 7.1 copy-start.14
  463.9 20.6 %slice-start = ((s8[12288000]{0:T(1024)(128)(4,1)}), s8[4194304]{0:T(1024)(128)(4,1)S(1)}, s32[]{:S(2)}) async-start(s8[12288000]{0:T(1024)(128)(4,1)} %bitcast.49), calls=%async_computation.4 | async-start | bytes 8388608
  464.0 20.6 %slice-start.1 = ((s8[12288000]{0:T(1024)(128)(4,1)}), s8[4194304]{0:T(1024)(128)(4,1)S(1)}, s32[]{:S(2)}) async-start(s8[12288000]{0:T(1024)(128)(4,1)} %bitcast.49), calls=%async_computation.5 | async-start | bytes 8388608
  472.5 12.1 %slice-start.2 = ((s8[12288000]{0:T(1024)(128)(4,1)}), s8[3899392]{0:T(1024)(128)(4,1)S(1)}, s32[]{:S(2)}) async-start(s8[12288000]{0:T(1024)(128)(4,1)} %bitcast.49), calls=%async_computation.6 | async-start | bytes 7798784
  510.6 11.9 %copy-start.12 = (bf16[10,197,6,64]{1,3,2,0:T(8,128)(2,1)S(1)}, bf16[10,197,6,64]{1,3,2,0:T(8,128)(2,1)}, u32[]{:S(2)}) copy-start(bf16[10,197,6,64]{1,3,2,0:T(8,128)(2,1)} %get-tuple-element.81) | copy-start | bytes 4538884
  526.8 9.3 copy-start.15
  526.8 11.8 copy-start.21
  526.8 11.8 copy-start.23
  526.8 11.8 copy-start.25
  526.8 11.8 copy-start.35
  547.8 537.8 %all-reduce.14.cloned.1.call-start = ((), (), s32[]{:S(2)}) async-start(), calls=%async_computation.3 | async-start | bytes 24281088 | tf_op jit(solution)/shard_map/psum | solution.py:102
  547.8 11.2 copy-start.19
  547.8 11.2 copy-start.31
  1109.1 65.9 %copy-start.17 = (f32[384,768]{1,0:T(8,128)S(1)}, f32[384,768]{1,0:T(8,128)}, u32[]{:S(2)}) copy-start(f32[384,768]{1,0:T(8,128)} %get-tuple-element.92) | copy-start | bytes 3538948
  1113.3 67.8 %slice-start.3 = ((s8[4718592]{0:T(1024)(128)(4,1)}), s8[524288]{0:T(1024)(128)(4,1)S(1)}, s32[]{:S(2)}) async-start(s8[4718592]{0:T(1024)(128)(4,1)} %bitcast.51), calls=%async_computation.7 | async-start | bytes 1048576
  1176.0 7.2 copy-start.1
  (15 other events, 53.6 us)
Sparse Core Ops, SparseCore 0:
  103.9 151.1 all-reduce.7
  288.2 148.9 all-reduce.9
  547.9 256.6 all-reduce.11
  806.9 278.5 all-reduce.13
where the time goes:
time: 1200 us; the launch traced here: 1190 us
  waiting for transfers between devices  789 us (66%)
  local copies, waits for them, and re-layouts  135 us (11%)
  matrix products  127 us (11%)
  blocking collectives  61.7 us (5%)
  other arithmetic  61 us (5%)
  between operations  15.2 us (1%)
    psum x1, waiting for transfers between devices, shards(): mlp_full = lax.psum(mlp_part, 'tensor')  276 us
    psum x1, waiting for transfers between devices, shards(): lax.psum((first_norm_gain_gradient, grad_ln1_bias, grad_w_qkv, grad_qv_bi...  237 us
    psum x1, waiting for transfers between devices, shards(): attn_full = lax.psum(attn_part, 'tensor')  147 us
    psum x1, waiting for transfers between devices, shards(): second_normed_gradient = lax.psum(norm_two_part, 'tensor')  130 us
    psum x1, blocking collectives, shards(): lax.psum((first_norm_gain_gradient, grad_ln1_bias, grad_w_qkv, grad_qv_bi...  61.7 us
    another operation x7, local copies, waits for them, and re-layouts, shards(): jnp.stack([grad_queries, grad_keys, grad_values])  34.4 us
    unnamed x92, local copies, waits for them, and re-layouts  24.3 us
  transfers between devices with their start and end apart: 4, of which 4 were waited for; matrix products, arithmetic and copies ran while one was open for 4% of the time, Pallas kernels for 0%

commit v1 on v0

--- a/solution.py
+++ b/solution.py
@@ -90,7 +90,7 @@
         .reshape(total_rows, local_width)
     )
     attn_part = jnp.dot(context, w_out, preferred_element_type=float_thirtytwo)
-    attn_full = lax.psum(attn_part, "tensor")
+    attn_full = attn_part + lax.ppermute(attn_part, "tensor", [(0, 1), (1, 0)])
     residual_stream = input_tokens + (attn_full + b_out)
     second_normed_tokens, second_centered_scaled, second_inverse_deviation = apply_layer_norm(
         residual_stream, second_norm_gain, second_norm_bias

time: 1200 us -> 1190 us (level)
  waiting for transfers between devices: 789 us -> 770 us
    psum x1 -> x0, waiting for transfers between devices: 147 us -> none  [shards(): attn_full = lax.psum(attn_part, 'tensor')]
    ppermute x0 -> x1, waiting for transfers between devices: none -> 126 us  [shards(): attn_full = attn_part + lax.ppermute(attn_part, 'tensor', [(0, 1), (1, 0)])]
where the time goes in v1:
time: 1190 us; the launch traced here: 1180 us
  waiting for transfers between devices  770 us (65%)
  local copies, waits for them, and re-layouts  136 us (11%)
  matrix products  128 us (11%)
  other arithmetic  68.2 us (6%)
  blocking collectives  61.7 us (5%)
  between operations  15.1 us (1%)
    psum x1, waiting for transfers between devices, shards(): mlp_full = lax.psum(mlp_part, 'tensor')  276 us
    psum x1, waiting for transfers between devices, shards(): lax.psum((first_norm_gain_gradient, grad_ln1_bias, grad_w_qkv, grad_qv_bi...  237 us
    psum x1, waiting for transfers between devices, shards(): second_normed_gradient = lax.psum(norm_two_part, 'tensor')  131 us
    ppermute x1, waiting for transfers between devices, shards(): attn_full = attn_part + lax.ppermute(attn_part, 'tensor', [(0, 1), (1, 0)])  126 us
    psum x1, blocking collectives, shards(): lax.psum((first_norm_gain_gradient, grad_ln1_bias, grad_w_qkv, grad_qv_bi...  61.7 us
    another operation x7, local copies, waits for them, and re-layouts, shards(): jnp.stack([grad_queries, grad_keys, grad_values])  34.4 us
    unnamed x92, local copies, waits for them, and re-layouts  25 us
  transfers between devices with their start and end apart: 4, of which 4 were waited for; matrix products, arithmetic and copies ran while one was open for 4% of the time, Pallas kernels for 0%

profile of v1, /device:TPU:0, one launch (start us, length us, event | category | flops | bytes accessed | tf_op | source)
XLA Modules:
  0.0 1182.2 jit_solution(8866942042955673046)
XLA Ops:
  7.3 6.9 reshape.188
  19.7 7.4 convolution_bitcast_fusion
  35.0 8.1 squeeze.14
  68.9 8.1 squeeze.13
  80.2 8.9 convert_bitcast_fusion.1
  92.1 5.9 reshape.183
  98.0 5.8 fusion.37
  111.5 126.4 %collective-permute-done = f32[1970,768]{1,0:T(8,128)} collective-permute-done((f32[1970,768]{1,0:T(8,128)}, f32[1970,768]{1,0:T(8,128)}, u32[]{:S(2)}, u32[]{:S(2)}) %collective-permute-start) | collective-permute-done | bytes 6051872 | tf_op jit(solution)/shard_map/ppermute | solution.py:93
  237.9 9.7 fusion.35
  252.1 8.1 multiply_convert_fusion.1
  260.1 9.6 convert_reduce_fusion
  272.3 6.8 fusion.39
  279.2 10.1 fusion.29
  289.3 8.9 fusion.32
  298.2 131.0 %all-reduce.7.cloned.1.call-done = f32[1970,768]{1,0:T(8,128)} async-done(((f32[1970,768]{1,0:T(8,128)}), f32[1970,768]{1,0:T(8,128)}) %all-reduce.7.cloned.1.call-update) | async-done | bytes 6051856 | tf_op jit(solution)/shard_map/psum | solution.py:125
  429.2 6.0 multiply_reduce_fusion.3
  456.0 8.5 convert_reduce_fusion.2
  464.5 12.1 %multiply_reduce_fusion = (f32[10,6,197]{2,1,0:T(8,128)S(1)}, f32[10,6,197,197]{2,3,1,0:T(8,128)}) fusion(f32[10,6,197,197]{2,3,1,0:T(8,128)} %copy-done.2, f32[10,6,197]{2,1,0:T(8,128)S(1)} %log_add_fusion, bf16[10,197,6,64]{1,3,2,0:T(8,128)(2,1)S(1)} %copy.49, bf16[10,197,6,64]{1,0,3,2:T(8,128)(2,1)} %copy-done.11), kind=kOutput, calls=%fused_computation.2 | convolution fusion | flops 307355456 | bytes 21748800 | tf_op jit(solution)/shard_map/ishd,ithd->ihst/dot_general | solution.py:146
  476.6 6.5 multiply_convert_fusion
  496.7 6.0 reshape.193
  502.7 5.9 copy.69
  508.6 6.0 reshape.192
  518.9 6.1 reshape.191
  530.7 9.1 convolution_bitcast_fusion.2
  539.9 11.2 fusion.38
  551.1 6.2 convolution_bitcast_fusion.1
  559.8 236.9 %all-reduce.9.cloned.1.call-done = (f32[3,768,384]{1,2,0:T(8,128)}, f32[384,768]{1,0:T(8,128)}, f32[768,1536]{1,0:T(8,128)}, f32[1536,768]{1,0:T(8,128)}) async-done(((f32[3,768,384]{1,2,0:T(8,128)}, f32[384,768]{1,0:T(8,128)}, f32[768,1536]{1,0:T(8,128)}, f32[1536,768]{1,0:T(8,128)}), (f32[3,768,384]{1,2,0:T(8,128)}, f32[384,768]{1,0:T(8,128)}, f32[768,1536]{1,0:T(8,128)}, ...) | async-done | bytes 14155792 | tf_op jit(solution)/shard_map/psum | solution.py:190
  801.8 276.0 %all-reduce.11.cloned.1.call-done = (f32[1970,768]{1,0:T(8,128)}, f32[1970,768]{1,0:T(8,128)}) async-done(((f32[1970,768]{1,0:T(8,128)}, f32[1970,768]{1,0:T(8,128)}), (f32[1970,768]{1,0:T(8,128)}, f32[1970,768]{1,0:T(8,128)})) %all-reduce.11.cloned.1.call-update) | async-done | bytes 12103696 | tf_op jit(solution)/shard_map/psum | solution.py:102
  1077.8 5.9 multiply_reduce_fusion.4
  1084.0 6.7 add_convert_fusion.2
  1094.8 6.6 select_convert_fusion
  1105.5 61.7 %all-reduce = (f32[768]{0:T(1024)}, f32[768]{0:T(1024)}, f32[2,384]{1,0:T(2,128)}, f32[768]{0:T(1024)}, f32[768]{0:T(1024)}, /*index=5*/f32[768]{0:T(1024)}, f32[1536]{0:T(1024)}, f32[768]{0:T(1024)}) all-reduce(f32[768]{0:T(1024)S(1)} %get-tuple-element.44, ...), channel_id=1, replica_groups=mesh['dp'=16,'tensor'=2] {'dp'}, use_global_device_ids=true, to_apply=%region_15.16 | all-reduce | flops 6912 | bytes 55296 | tf_op jit(solution)/shard_map/psum | solution.py:190
  (148 shorter events, 128.1 us)
Async XLA Ops:
  7.2 244.1 %copy-start = (bf16[768,1536]{1,0:T(8,128)(2,1)S(1)}, bf16[768,1536]{1,0:T(8,128)(2,1)}, u32[]{:S(2)}) copy-start(bf16[768,1536]{1,0:T(8,128)(2,1)} %param.25) | copy-start | bytes 7077892
  7.2 12.5 %copy-start.24 = (f32[768]{0:T(1024)S(1)}, f32[768]{0:T(1024)}, u32[]{:S(2)}) copy-start(f32[768]{0:T(1024)} %param.17) | copy-start | bytes 9220
  7.2 12.5 %copy-start.34 = (f32[768]{0:T(1024)S(1)}, f32[768]{0:T(1024)}, u32[]{:S(2)}) copy-start(f32[768]{0:T(1024)} %param.18) | copy-start | bytes 9220
  7.2 422.0 %all-reduce.7.cloned.1.call-start = ((), (), s32[]{:S(2)}) async-start(), calls=%async_computation | async-start | bytes 12140544 | tf_op jit(solution)/shard_map/psum | solution.py:125
  19.5 7.6 copy-start.20
  19.7 7.5 copy-start.22
  35.0 8.1 copy-start.29
  80.1 8.9 copy-start.11
  89.0 9.0 copy-start.16
  98.0 139.9 %copy-start.27 = (f32[768]{0:T(1024)S(1)}, f32[768]{0:T(1024)}, u32[]{:S(2)}) copy-start(f32[768]{0:T(1024)} %param.22) | copy-start | bytes 9220
  103.8 134.1 %collective-permute-start = (f32[1970,768]{1,0:T(8,128)}, f32[1970,768]{1,0:T(8,128)}, u32[]{:S(2)}, u32[]{:S(2)}) collective-permute-start(f32[1970,768]{1,0:T(8,128)} %fusion.37), channel_id=1, source_target_pairs={{0,1},{1,0},{2,3},{3,2},{4,5},{5,4},{6,7},{7,6},{8,9},{9,8},{10,11... | collective-permute-start | bytes 18155528 | tf_op jit(solution)/shard_map/ppermute | solution.py:93
  252.0 8.1 copy-start.13
  252.0 8.1 copy-start.30
  279.1 517.5 %all-reduce.9.cloned.1.call-start = ((), (), s32[]{:S(2)}) async-start(), calls=%async_computation.1 | async-start | bytes 28311552 | tf_op jit(solution)/shard_map/psum | solution.py:190
  279.2 10.2 copy-start.37
  429.2 6.2 copy-start.8
  429.2 7.1 copy-start.14
  456.0 20.6 %slice-start = ((s8[12288000]{0:T(1024)(128)(4,1)}), s8[4194304]{0:T(1024)(128)(4,1)S(1)}, s32[]{:S(2)}) async-start(s8[12288000]{0:T(1024)(128)(4,1)} %bitcast.49), calls=%async_computation.3 | async-start | bytes 8388608
  456.0 20.6 %slice-start.1 = ((s8[12288000]{0:T(1024)(128)(4,1)}), s8[4194304]{0:T(1024)(128)(4,1)S(1)}, s32[]{:S(2)}) async-start(s8[12288000]{0:T(1024)(128)(4,1)} %bitcast.49), calls=%async_computation.4 | async-start | bytes 8388608
  464.5 12.1 %slice-start.2 = ((s8[12288000]{0:T(1024)(128)(4,1)}), s8[3899392]{0:T(1024)(128)(4,1)S(1)}, s32[]{:S(2)}) async-start(s8[12288000]{0:T(1024)(128)(4,1)} %bitcast.49), calls=%async_computation.5 | async-start | bytes 7798784
  502.7 11.9 %copy-start.12 = (bf16[10,197,6,64]{1,3,2,0:T(8,128)(2,1)S(1)}, bf16[10,197,6,64]{1,3,2,0:T(8,128)(2,1)}, u32[]{:S(2)}) copy-start(bf16[10,197,6,64]{1,3,2,0:T(8,128)(2,1)} %get-tuple-element.81) | copy-start | bytes 4538884
  518.9 9.3 copy-start.15
  518.9 11.8 copy-start.21
  518.9 11.8 copy-start.23
  518.9 11.8 copy-start.25
  518.9 11.8 copy-start.35
  539.8 538.0 %all-reduce.11.cloned.1.call-start = ((), (), s32[]{:S(2)}) async-start(), calls=%async_computation.2 | async-start | bytes 24281088 | tf_op jit(solution)/shard_map/psum | solution.py:102
  539.9 11.2 copy-start.19
  539.9 11.2 copy-start.31
  1101.3 65.9 %copy-start.17 = (f32[384,768]{1,0:T(8,128)S(1)}, f32[384,768]{1,0:T(8,128)}, u32[]{:S(2)}) copy-start(f32[384,768]{1,0:T(8,128)} %get-tuple-element.92) | copy-start | bytes 3538948
  1105.5 67.8 %slice-start.3 = ((s8[4718592]{0:T(1024)(128)(4,1)}), s8[524288]{0:T(1024)(128)(4,1)S(1)}, s32[]{:S(2)}) async-start(s8[4718592]{0:T(1024)(128)(4,1)} %bitcast.51), calls=%async_computation.6 | async-start | bytes 1048576
  1168.2 7.2 copy-start.1
  (15 other events, 62.6 us)
Sparse Core Ops, SparseCore 0:
  279.2 149.9 all-reduce.6
  539.9 256.6 all-reduce.8
  799.1 278.5 all-reduce.10
